TPU v7x, 32 devices: a whole 2x2x4 slice. The times are simulated.
32 devices in a mesh: dp: 4 (over z), ctx: 4 (over y, core), tensor: 2 (over x).
Axes of the slice: x: 2, y: 2, z: 4, core: 2. Of those that a mesh axis runs over, the one named last changes fastest.
Arguments:
- hidden_in: bfloat16 [4, 1024, 2048], P('dp', 'ctx'), may hold values from -6 to 6
- attn_norm_gain: float32 [2048], replicated, may hold values from 0.5 to 1.5
- attn_norm_bias: float32 [2048], replicated, may hold values from -2 to 2
- qkv_weight: bfloat16 [2048, 6144], P(None, 'tensor'), may hold values from -0.125 to 0.125
- qkv_bias: float32 [6144], P('tensor'), may hold values from -1.2 to 1.2
- dense_weight: bfloat16 [2048, 2048], P('tensor'), may hold values from -2 to 2
- dense_bias: float32 [2048], replicated, may hold values from -3 to 3
- mlp_norm_gain: float32 [2048], replicated, may hold values from 0.5 to 1.5
- mlp_norm_bias: float32 [2048], replicated, may hold values from -2 to 2
- up_weight: bfloat16 [2048, 8192], P(None, 'tensor'), may hold values from -0.125 to 0.125
- up_bias: float32 [8192], P('tensor'), may hold values from -3 to 3
- down_weight: bfloat16 [8192, 2048], P('tensor'), may hold values from -0.0625 to 0.0625
- down_bias: float32 [2048], replicated, may hold values from -3 to 3
- out_cotangent: bfloat16 [4, 1024, 2048], P('dp', 'ctx'), may hold values from -6 to 6
- subset_ids: int32 [4, 1024], P('dp', 'ctx'), may hold values from 0 to 21
- subset_weights: float32 [22], replicated, may hold values from 0.5 to 2
Outputs:
- layer_out: bfloat16 [4, 1024, 2048], P('dp', 'ctx')
- input_grad: bfloat16 [4, 1024, 2048], P('dp', 'ctx')
- grad_attn_norm_gain: float32 [2048], replicated
- grad_attn_norm_bias: float32 [2048], replicated
- grad_qkv_weight: float32 [2048, 6144], P(('dp', 'ctx'), 'tensor')
- grad_qkv_bias: float32 [6144], P('tensor')
- grad_dense_weight: float32 [2048, 2048], P('tensor', ('dp', 'ctx'))
- grad_dense_bias: float32 [2048], replicated
- grad_mlp_norm_gain: float32 [2048], replicated
- grad_mlp_norm_bias: float32 [2048], replicated
- grad_up_weight: float32 [2048, 8192], P(('dp', 'ctx'), 'tensor')
- grad_up_bias: float32 [8192], P('tensor')
- grad_down_weight: float32 [8192, 2048], P('tensor', ('dp', 'ctx'))
- grad_down_bias: float32 [2048], replicated
Inputs may be any that keep to these rules, and one draw needn't show every extreme that they name: `subset_ids`: the corpus subset of every token, one of 22.
All inputs are finite; a program needn't handle non-finite values.
Results may differ from a plain program's by a relative error of at most 0.012.
Values may be sent and summed in bfloat16 or wider, within the bound.
A program may use at most 256 MiB of HBM per device.

v0:
```python
import math
import jax
import jax.numpy as jnp
from jax import lax
from jax.sharding import PartitionSpec as P

HS = 256
ROT = 64
NORM_EPS = 1e-05


def rope_tables(positions, rot_dims):
    half_dims = rot_dims // 2
    freqs = 10000.0 ** (-(jnp.arange(half_dims, dtype=jnp.float32) * 2.0 / rot_dims))
    angles = positions.astype(jnp.float32)[:, None] * freqs[None, :]
    return (
        jnp.concatenate([jnp.cos(angles), jnp.cos(angles)], -1),
        jnp.concatenate([jnp.sin(angles), jnp.sin(angles)], -1),
    )


def rotate(columns, cosine_table, sine_table):
    half_dims = ROT // 2
    leading = columns[..., :ROT]
    turned = jnp.concatenate([-leading[..., half_dims:], leading[..., :half_dims]], -1)
    moved = leading * cosine_table[:, None, :] + turned * sine_table[:, None, :]
    return jnp.concatenate([moved, columns[..., ROT:]], -1)


def rotate_back(gradient, cosine_table, sine_table):
    half_dims = ROT // 2
    leading = gradient[..., :ROT]
    scaled = leading * sine_table[:, None, :]
    turned = jnp.concatenate([scaled[..., half_dims:], -scaled[..., :half_dims]], -1)
    moved = leading * cosine_table[:, None, :] + turned
    return jnp.concatenate([moved, gradient[..., ROT:]], -1)


def swap(array, axis, bit):
    pairs = [(place, place ^ bit) for place in range(lax.axis_size(axis))]
    return lax.ppermute(array, axis, pairs)


def bits_down(axis):
    size = lax.axis_size(axis)
    return [1 << level for level in reversed(range(size.bit_length() - 1))]


def relative_blocks(array, axis, dim):
    place = lax.axis_index(axis)
    for bit in bits_down(axis):
        size = array.shape[dim]
        halves = array.reshape(
            array.shape[:dim] + (size // (2 * bit), 2, bit) + array.shape[dim + 1 :]
        )
        flipped = jnp.flip(halves, dim + 1)
        array = jnp.where(place & bit != 0, flipped, halves).reshape(array.shape)
    return array


def gather_rows(rows, axis):
    for bit in bits_down(axis):
        rows = jnp.concatenate([rows, swap(rows, axis, bit)], 0)
    return rows


def exchange_rows(rows, axis):
    for bit in bits_down(axis):
        rows = jnp.concatenate([rows[:, :bit], swap(rows[:, bit:], axis, bit)], 0)
    return rows[:, 0]


def block_order(size):
    order = [0]
    bit = size // 2
    while bit:
        order = order + [entry ^ bit for entry in order]
        bit //= 2
    return order


def tensor_sum(part):
    if lax.axis_size("tensor") == 2:
        low = part.astype(jnp.bfloat16)
        return low.astype(jnp.float32) + swap(low, "tensor", 1).astype(jnp.float32)
    return lax.psum(part, "tensor")


def reduce_line(left, right, spec, dim):
    size = lax.axis_size("dp")
    width = left.shape[1] // size
    arrived = None
    bits = [1 << level for level in range(size.bit_length() - 1)]
    count = size
    total = None
    for bit in bits:
        count //= 2
        if total is None:
            send = jnp.einsum(
                spec, left[:, count * width :], right, preferred_element_type=jnp.float32
            )
            keep = jnp.einsum(
                spec, left[:, : count * width], right, preferred_element_type=jnp.float32
            )
        else:
            keep = lax.slice_in_dim(total, 0, count * width, axis=dim)
            send = lax.slice_in_dim(total, count * width, 2 * count * width, axis=dim)
        arrived = swap(send.astype(jnp.bfloat16), "dp", bit)
        total = keep + arrived.astype(jnp.float32)
    return total


def reduce_blocks(total, axis, dim, bits=None):
    size = lax.axis_size(axis)
    for bit in [1 << level for level in range(size.bit_length() - 1)]:
        half = total.shape[dim] // 2
        keep = lax.slice_in_dim(total, 0, half, axis=dim)
        send = lax.slice_in_dim(total, half, 2 * half, axis=dim)
        arrived = swap(send.astype(jnp.bfloat16), axis, bit)
        total = keep + arrived.astype(jnp.float32)
    return total


def spread_columns(rows):
    dp_size, ctx_size = (lax.axis_size("dp"), lax.axis_size("ctx"))
    width = rows.shape[1] // (dp_size * ctx_size)
    blocks = rows.reshape(rows.shape[0], dp_size, ctx_size, width)
    blocks = relative_blocks(relative_blocks(blocks, "dp", 1), "ctx", 2)
    blocks = jnp.stack([blocks[:, entry] for entry in block_order(dp_size)], 2)
    return blocks.reshape(rows.shape[0], ctx_size, dp_size * width)


def local(
    hidden_in,
    attn_norm_gain,
    attn_norm_bias,
    qkv_weight,
    qkv_bias,
    dense_weight,
    dense_bias,
    mlp_norm_gain,
    mlp_norm_bias,
    up_weight,
    up_bias,
    down_weight,
    down_bias,
    out_cotangent,
    subset_ids,
    subset_weights,
):
    seq_count, block_len, model_width = hidden_in.shape
    row_count = seq_count * block_len
    head_count = qkv_weight.shape[1] // (3 * HS)
    ctx_size = lax.axis_size("ctx")
    length = block_len * ctx_size
    score_scale = 1.0 / math.sqrt(HS)
    low_type = jnp.bfloat16
    hidden_rows = hidden_in.reshape(row_count, model_width)
    inputs = hidden_rows.astype(jnp.float32)
    row_mean = jnp.mean(inputs, -1, keepdims=True)
    centered = inputs - row_mean
    inv_std = lax.rsqrt(jnp.mean(centered * centered, -1, keepdims=True) + NORM_EPS)
    normed = centered * inv_std
    attn_in = (normed * attn_norm_gain + attn_norm_bias).astype(low_type)
    mlp_in = (normed * mlp_norm_gain + mlp_norm_bias).astype(low_type)
    subset_count = subset_weights.shape[0]
    matches = subset_ids[..., None] == jnp.arange(subset_count, dtype=jnp.int32)
    row_weight = jnp.sum(jnp.where(matches, subset_weights, 0.0), -1).reshape(row_count, 1)
    grad_out = out_cotangent.reshape(row_count, model_width).astype(jnp.float32) * row_weight
    grad_low = grad_out.astype(low_type)
    grad_out_bias = jnp.sum(grad_out, 0)
    low_part = exchange_rows(spread_columns(grad_low), "ctx")
    hidden_part = exchange_rows(spread_columns(hidden_rows), "ctx").astype(jnp.float32)
    stats = gather_rows(jnp.stack([row_mean[:, 0], inv_std[:, 0]])[None], "ctx")
    mean_all = stats[:, 0].reshape(ctx_size * row_count, 1)
    std_all = stats[:, 1].reshape(ctx_size * row_count, 1)
    normed_part = (hidden_part - mean_all) * std_all

    def own_columns(vector):
        return spread_columns(vector[None])[:, 0]

    mlp_part = (normed_part * own_columns(mlp_norm_gain) + own_columns(mlp_norm_bias)).astype(
        low_type
    )
    attn_part = (normed_part * own_columns(attn_norm_gain) + own_columns(attn_norm_bias)).astype(
        low_type
    )
    hidden_units = up_weight.shape[1]
    pieces = max(1, hidden_units // 1024)
    span = hidden_units // pieces
    down_grads, up_grads, up_bias_parts = ([], [], [])
    branch_part, grad_mlp_in = (None, None)
    for piece in range(pieces):
        cols = slice(piece * span, (piece + 1) * span)
        up_pre = (
            jnp.dot(mlp_in, up_weight[:, cols], preferred_element_type=jnp.float32) + up_bias[cols]
        )
        activated = jax.nn.gelu(up_pre, approximate=False).astype(low_type)
        activated_all = gather_rows(activated, "ctx")
        down_grads.append(reduce_line(low_part, activated_all, "rd,rf->fd", 1))
        grad_act = jnp.einsum(
            "rd,fd->rf", grad_low, down_weight[cols], preferred_element_type=jnp.float32
        )
        gelu_back = jax.vjp(lambda pre_act: jax.nn.gelu(pre_act, approximate=False), up_pre)[1]
        grad_pre = gelu_back(grad_act)[0].astype(low_type)
        grad_pre_all = gather_rows(grad_pre, "ctx")
        up_grads.append(reduce_line(mlp_part, grad_pre_all, "rd,rf->df", 0))
        up_bias_parts.append(jnp.sum(grad_pre.astype(jnp.float32), 0))
        more = jnp.dot(activated, down_weight[cols], preferred_element_type=jnp.float32)
        branch_part = more if branch_part is None else branch_part + more
        more = jnp.einsum(
            "rf,df->rd", grad_pre, up_weight[:, cols], preferred_element_type=jnp.float32
        )
        grad_mlp_in = more if grad_mlp_in is None else grad_mlp_in + more
    qkv_all = jnp.dot(attn_in, qkv_weight, preferred_element_type=jnp.float32) + qkv_bias
    qkv_all = qkv_all.reshape(seq_count, block_len, head_count, 3, HS)
    place = lax.axis_index("ctx")
    steps = jnp.arange(block_len, dtype=jnp.int32)
    positions = place * block_len + steps
    cosine_table, sine_table = rope_tables(positions, ROT)
    query_rows = rotate(qkv_all[:, :, :, 0], cosine_table, sine_table).astype(low_type)
    key_rows = rotate(qkv_all[:, :, :, 1], cosine_table, sine_table).astype(low_type)
    value_rows = qkv_all[:, :, :, 2].astype(low_type)
    pair = jnp.stack([key_rows, value_rows], 0).reshape(2 * seq_count, block_len, head_count * HS)
    whole = gather_rows(jnp.swapaxes(pair, 0, 1), "ctx")
    whole = jnp.swapaxes(whole, 0, 1).reshape(2, seq_count, length, head_count, HS)
    key_whole, value_whole = (whole[0], whole[1])
    key_positions = jnp.concatenate(
        [(place ^ entry) * block_len + steps for entry in block_order(ctx_size)]
    )
    causal = key_positions[None, :] <= positions[:, None]
    raw = jnp.einsum("sqhd,skhd->shqk", query_rows, key_whole, preferred_element_type=jnp.float32)
    scores = jnp.where(causal, raw * score_scale, -1e30)
    row_max = jnp.max(scores, -1, keepdims=True)
    expd = jnp.exp(scores - row_max)
    prob = expd / jnp.sum(expd, -1, keepdims=True)
    prob_low = prob.astype(low_type)
    attn_out = jnp.einsum(
        "shqk,skhd->sqhd", prob_low, value_whole, preferred_element_type=jnp.float32
    ).astype(low_type)
    attn_out = attn_out.reshape(row_count, head_count * HS)
    attn_out_all = gather_rows(attn_out, "ctx")
    grad_dense_weight = reduce_line(low_part, attn_out_all, "rd,rf->fd", 1)
    branch_part = branch_part + jnp.dot(attn_out, dense_weight, preferred_element_type=jnp.float32)
    layer_out = (inputs + tensor_sum(branch_part) + dense_bias + down_bias).astype(low_type)
    layer_out = layer_out.reshape(seq_count, block_len, model_width)
    grad_attn = jnp.einsum("rd,kd->rk", grad_low, dense_weight, preferred_element_type=jnp.float32)
    grad_attn = grad_attn.astype(low_type).reshape(seq_count, block_len, head_count, HS)
    grad_prob = jnp.einsum(
        "sqhd,skhd->shqk", grad_attn, value_whole, preferred_element_type=jnp.float32
    )
    delta = jnp.sum(grad_prob * prob, -1, keepdims=True)
    grad_scores = (prob * (grad_prob - delta)).astype(low_type)
    grad_query = (
        jnp.einsum("shqk,skhd->sqhd", grad_scores, key_whole, preferred_element_type=jnp.float32)
        * score_scale
    )
    grad_key_whole = (
        jnp.einsum("shqk,sqhd->kshd", grad_scores, query_rows, preferred_element_type=jnp.float32)
        * score_scale
    )
    grad_value_whole = jnp.einsum(
        "shqk,sqhd->kshd", prob_low, grad_attn, preferred_element_type=jnp.float32
    )
    grad_pair = jnp.concatenate(
        [
            grad_key_whole.reshape(length, seq_count * head_count * HS),
            grad_value_whole.reshape(length, seq_count * head_count * HS),
        ],
        1,
    )
    grad_pair = reduce_blocks(grad_pair, "ctx", 0)
    grad_pair = grad_pair.reshape(block_len, 2, seq_count, head_count, HS)
    grad_key_rows = jnp.swapaxes(grad_pair[:, 0], 0, 1)
    grad_value_rows = jnp.swapaxes(grad_pair[:, 1], 0, 1)
    grad_qkv = jnp.stack(
        [
            rotate_back(grad_query, cosine_table, sine_table),
            rotate_back(grad_key_rows, cosine_table, sine_table),
            grad_value_rows,
        ],
        3,
    )
    grad_qkv = grad_qkv.reshape(row_count, head_count * 3 * HS).astype(low_type)
    qkv_grads = []
    for head in range(head_count):
        piece = grad_qkv[:, head * 3 * HS : (head + 1) * 3 * HS]
        qkv_grads.append(reduce_line(attn_part, gather_rows(piece, "ctx"), "rd,rc->dc", 0))
    grad_qkv_bias = jnp.sum(grad_qkv.astype(jnp.float32), 0)
    grad_attn_in = jnp.einsum("rc,dc->rd", grad_qkv, qkv_weight, preferred_element_type=jnp.float32)
    norm_parts = jnp.stack(
        [
            jnp.sum(grad_attn_in * normed, 0),
            jnp.sum(grad_attn_in, 0),
            jnp.sum(grad_mlp_in * normed, 0),
            jnp.sum(grad_mlp_in, 0),
        ]
    )
    grad_normed = grad_attn_in * attn_norm_gain + grad_mlp_in * mlp_norm_gain
    input_part = inv_std * (
        grad_normed
        - jnp.mean(grad_normed, -1, keepdims=True)
        - normed * jnp.mean(grad_normed * normed, -1, keepdims=True)
    )
    input_grad = (
        (grad_out + tensor_sum(input_part))
        .astype(low_type)
        .reshape(seq_count, block_len, model_width)
    )
    norm_total = lax.psum(norm_parts, ("dp", "ctx", "tensor"))
    qkv_bias_sum, up_bias_sum, out_bias_sum = lax.psum(
        (grad_qkv_bias, jnp.concatenate(up_bias_parts), grad_out_bias), ("dp", "ctx")
    )
    return (
        layer_out,
        input_grad,
        norm_total[0],
        norm_total[1],
        jnp.concatenate(qkv_grads, 1),
        qkv_bias_sum,
        grad_dense_weight,
        out_bias_sum,
        norm_total[2],
        norm_total[3],
        jnp.concatenate(up_grads, 1),
        up_bias_sum,
        jnp.concatenate(down_grads, 0),
        out_bias_sum,
    )


def solution(mesh):
    return jax.shard_map(
        local,
        mesh=mesh,
        in_specs=(
            P("dp", "ctx", None),
            P(),
            P(),
            P(None, "tensor"),
            P("tensor"),
            P("tensor", None),
            P(),
            P(),
            P(),
            P(None, "tensor"),
            P("tensor"),
            P("tensor", None),
            P(),
            P("dp", "ctx", None),
            P("dp", "ctx"),
            P(),
        ),
        out_specs=(
            P("dp", "ctx", None),
            P("dp", "ctx", None),
            P(),
            P(),
            P(("dp", "ctx"), "tensor"),
            P("tensor"),
            P("tensor", ("dp", "ctx")),
            P(),
            P(),
            P(),
            P(("dp", "ctx"), "tensor"),
            P("tensor"),
            P("tensor", ("dp", "ctx")),
            P(),
        ),
        check_vma=False,
    )
```

profile of v0, /device:TPU:0, one launch (start us, length us, event | category | flops | bytes accessed | tf_op | source)
XLA Modules:
  0.0 691.7 jit_solution(6590537447660785061)
XLA Ops:
  4.1 6.9 multiply_convert_fusion.5
  34.3 9.9 %convolution_add_fusion = f32[256,3072]{1,0:T(8,128)} fusion(bf16[2048,3072]{1,0:T(8,128)(2,1)} %param.19, f32[3072]{0:T(1024)S(1)} %copy-done.93, bf16[1,256,2048]{2,1,0:T(8,128)(2,1)S(1)} %copy-done, f32[2048]{0:T(1024)S(1)} %copy-done.67, f32[2048]{0:T(1024)S(1)} %copy-done.70, f32[256]{0:T(256)S(1)} %add_rsqrt_fusion, f32[256]{0:T(256)S(1)} %broadcast_multiply_fusion.2), kind=kOutput, calls=%fused_computation.12 | convolution fusion | flops 3225157632 | bytes 16807936 | tf_op jit(solution)/shard_map/dot_general | solution.py:215
  85.4 7.3 %convert_reduce_fusion.5 = (f32[1024]{0:T(1024)}, bf16[256,1024]{1,0:T(8,128)(2,1)}) fusion(f32[256,1024]{1,0:T(8,128)S(1)} %copy-done.94, bf16[4096,2048]{1,0:T(8,128)(2,1)} %param.27, bf16[1,256,2048]{2,1,0:T(8,128)(2,1)S(1)} %copy-done.3, f32[256]{0:T(256)S(1)} %fusion.188), kind=kOutput, calls=%fused_computation.202 | convolution fusion | flops 1094712320 | bytes 6820864 | tf_op jit(solution)/shard_map/rd,fd->rf/dot_general | solution.py:201
  158.5 20.1 %collective-permute-done.6 = bf16[256,2,512]{0,2,1:T(8,128)(2,1)S(1)} collective-permute-done((bf16[256,2,512]{0,2,1:T(8,128)(2,1)S(1)}, bf16[256,2,512]{0,2,1:T(8,128)(2,1)S(1)}, u32[]{:S(2)}, u32[]{:S(2)}) %collective-permute-start.6) | collective-permute-done | bytes 524320 | tf_op jit(solution)/shard_map/ppermute | solution.py:41
  178.7 11.0 %collective-permute-done.28 = bf16[256,2,512]{0,2,1:T(8,128)(2,1)S(1)} collective-permute-done((bf16[256,2,512]{0,2,1:T(8,128)(2,1)S(1)}, bf16[256,2,512]{0,2,1:T(8,128)(2,1)S(1)}, u32[]{:S(2)}, u32[]{:S(2)}) %collective-permute-start.28) | collective-permute-done | bytes 524320 | tf_op jit(solution)/shard_map/ppermute | solution.py:41
  191.4 9.6 %collective-permute-done.40 = bf16[256,1024]{1,0:T(8,128)(2,1)S(1)} collective-permute-done((bf16[256,1024]{1,0:T(8,128)(2,1)}, bf16[256,1024]{1,0:T(8,128)(2,1)S(1)}, u32[]{:S(2)}, u32[]{:S(2)}) %collective-permute-start.40) | collective-permute-done | bytes 524320 | tf_op jit(solution)/shard_map/ppermute | solution.py:41
  203.3 31.0 %collective-permute-done.44 = bf16[256,1024]{1,0:T(8,128)(2,1)S(1)} collective-permute-done((bf16[256,1024]{1,0:T(8,128)(2,1)S(1)}, bf16[256,1024]{1,0:T(8,128)(2,1)S(1)}, u32[]{:S(2)}, u32[]{:S(2)}) %collective-permute-start.44) | collective-permute-done | bytes 524320 | tf_op jit(solution)/shard_map/ppermute | solution.py:41
  270.6 7.4 %collective-permute-done.54 = bf16[1024,256]{1,0:T(8,128)(2,1)S(1)} collective-permute-done((bf16[1024,256]{1,0:T(8,128)(2,1)S(1)}, bf16[1024,256]{1,0:T(8,128)(2,1)S(1)}, u32[]{:S(2)}, u32[]{:S(2)}) %collective-permute-start.54) | collective-permute-done | bytes 524320 | tf_op jit(solution)/shard_map/ppermute | solution.py:41
  281.8 7.4 %collective-permute-done.58 = bf16[1024,256]{1,0:T(8,128)(2,1)S(1)} collective-permute-done((bf16[1024,256]{1,0:T(8,128)(2,1)S(1)}, bf16[1024,256]{1,0:T(8,128)(2,1)S(1)}, u32[]{:S(2)}, u32[]{:S(2)}) %collective-permute-start.58) | collective-permute-done | bytes 524320 | tf_op jit(solution)/shard_map/ppermute | solution.py:41
  293.2 7.3 %collective-permute-done.62 = bf16[1024,256]{1,0:T(8,128)(2,1)S(1)} collective-permute-done((bf16[1024,256]{1,0:T(8,128)(2,1)S(1)}, bf16[1024,256]{1,0:T(8,128)(2,1)S(1)}, u32[]{:S(2)}, u32[]{:S(2)}) %collective-permute-start.62) | collective-permute-done | bytes 524320 | tf_op jit(solution)/shard_map/ppermute | solution.py:41
  304.0 7.7 %collective-permute-done.34 = bf16[256,1024]{1,0:T(8,128)(2,1)S(1)} collective-permute-done((bf16[256,1024]{1,0:T(8,128)(2,1)S(1)}, bf16[256,1024]{1,0:T(8,128)(2,1)S(1)}, u32[]{:S(2)}, u32[]{:S(2)}) %collective-permute-start.34) | collective-permute-done | bytes 524320 | tf_op jit(solution)/shard_map/ppermute | solution.py:41
  316.3 12.3 %collective-permute-done.38 = bf16[256,1024]{1,0:T(8,128)(2,1)S(1)} collective-permute-done((bf16[256,1024]{1,0:T(8,128)(2,1)S(1)}, bf16[256,1024]{1,0:T(8,128)(2,1)S(1)}, u32[]{:S(2)}, u32[]{:S(2)}) %collective-permute-start.38) | collective-permute-done | bytes 524320 | tf_op jit(solution)/shard_map/ppermute | solution.py:41
  332.3 13.1 %collective-permute-done.42 = bf16[256,1024]{1,0:T(8,128)(2,1)S(1)} collective-permute-done((bf16[256,1024]{1,0:T(8,128)(2,1)S(1)}, bf16[256,1024]{1,0:T(8,128)(2,1)S(1)}, u32[]{:S(2)}, u32[]{:S(2)}) %collective-permute-start.42) | collective-permute-done | bytes 524320 | tf_op jit(solution)/shard_map/ppermute | solution.py:41
  348.9 7.1 %collective-permute-done.46 = bf16[256,1024]{1,0:T(8,128)(2,1)S(1)} collective-permute-done((bf16[256,1024]{1,0:T(8,128)(2,1)S(1)}, bf16[256,1024]{1,0:T(8,128)(2,1)S(1)}, u32[]{:S(2)}, u32[]{:S(2)}) %collective-permute-start.46) | collective-permute-done | bytes 524320 | tf_op jit(solution)/shard_map/ppermute | solution.py:41
  364.0 21.9 %collective-permute-done.59 = bf16[1024,128]{1,0:T(8,128)(2,1)S(1)} collective-permute-done((bf16[1024,128]{1,0:T(8,128)(2,1)S(1)}, bf16[1024,128]{1,0:T(8,128)(2,1)S(1)}, u32[]{:S(2)}, u32[]{:S(2)}) %collective-permute-start.59) | collective-permute-done | bytes 262176 | tf_op jit(solution)/shard_map/ppermute | solution.py:41
  386.0 11.2 %collective-permute-done.63 = bf16[1024,128]{1,0:T(8,128)(2,1)S(1)} collective-permute-done((bf16[1024,128]{1,0:T(8,128)(2,1)S(1)}, bf16[1024,128]{1,0:T(8,128)(2,1)S(1)}, u32[]{:S(2)}, u32[]{:S(2)}) %collective-permute-start.63) | collective-permute-done | bytes 262176 | tf_op jit(solution)/shard_map/ppermute | solution.py:41
  397.2 11.2 %collective-permute-done.35 = bf16[128,1024]{1,0:T(8,128)(2,1)S(1)} collective-permute-done((bf16[128,1024]{1,0:T(8,128)(2,1)S(1)}, bf16[128,1024]{1,0:T(8,128)(2,1)S(1)}, u32[]{:S(2)}, u32[]{:S(2)}) %collective-permute-start.35) | collective-permute-done | bytes 262176 | tf_op jit(solution)/shard_map/ppermute | solution.py:41
  420.8 8.5 %collective-permute-done.26 = bf16[256,1024]{0,1:T(8,128)(2,1)S(1)} collective-permute-done((bf16[256,1024]{0,1:T(8,128)(2,1)S(1)}, bf16[256,1024]{0,1:T(8,128)(2,1)S(1)}, u32[]{:S(2)}, u32[]{:S(2)}) %collective-permute-start.26) | collective-permute-done | bytes 524320 | tf_op jit(solution)/shard_map/ppermute | solution.py:41
  451.6 12.3 %collective-permute-done.31 = bf16[1024,128]{1,0:T(8,128)(2,1)S(1)} collective-permute-done((bf16[1024,128]{1,0:T(8,128)(2,1)S(1)}, bf16[1024,128]{1,0:T(8,128)(2,1)S(1)}, u32[]{:S(2)}, u32[]{:S(2)}) %collective-permute-start.31) | collective-permute-done | bytes 262176 | tf_op jit(solution)/shard_map/ppermute | solution.py:41
  478.2 9.7 %fusion.236 = (f32[256]{0:T(256)S(1)}, f32[256]{0:T(256)S(1)}, f32[2048]{0:T(1024)S(1)}, f32[2048]{0:T(1024)S(1)}, f32[2048]{0:T(1024)S(1)}, /*index=5*/f32[2048]{0:T(1024)S(1)}, f32[256,2048]{1,0:T(8,128)S(1)}) fusion(f32[256]{0:T(256)S(1)} %copy-done.62, f32[256]{0:T(256)S(1)} %copy-done.54, bf16[1,256,2048]{2,1,0:T(8,128)(2,1)S(1)} %copy-done.1, ...), kind=kOutput, calls=%fused_computation.457 | convolution fusion | flops 3229081088 | bytes 19451904 | tf_op jit(solution)/shard_map/rc,dc->rd/dot_general | solution.py:290
  498.3 59.7 %psum.28 = f32[4,2048]{1,0:T(4,128)S(1)} all-reduce(f32[4,2048]{1,0:T(4,128)S(1)} %pad_maximum_fusion.68), channel_id=1, replica_groups=mesh['dp'=4,'ctx'=4,'tensor'=2] {'dp','ctx','tensor'}, use_global_device_ids=true, to_apply=%region_12.13 | all-reduce | flops 8192 | bytes 65536 | tf_op jit(solution)/shard_map/psum | solution.py:310
  568.9 61.6 %all-reduce = (f32[3072]{0:T(1024)}, f32[2048]{0:T(1024)S(1)}, f32[4096]{0:T(1024)}) all-reduce(f32[3072]{0:T(1024)S(1)} %reduce_sum.167, f32[2048]{0:T(1024)S(1)} %get-tuple-element.40, f32[4096]{0:T(1024)S(1)} %pad_maximum_fusion.69), channel_id=1, replica_groups=mesh['dp'=4,'ctx'=4,'tensor'=2] {'dp','ctx'}, use_global_device_ids=true, to_apply=%region_14.15 | all-reduce | flops 9216 | bytes 73728 | tf_op jit(solution)/shard_map/psum | solution.py:311
  648.9 10.6 %collective-permute-done.16 = bf16[256,768]{1,0:T(8,128)(2,1)S(1)} collective-permute-done((bf16[256,768]{1,0:T(8,128)(2,1)S(1)}, bf16[256,768]{1,0:T(8,128)(2,1)S(1)}, u32[]{:S(2)}, u32[]{:S(2)}) %collective-permute-start.16) | collective-permute-done | bytes 393248 | tf_op jit(solution)/shard_map/ppermute | solution.py:41
  673.4 9.9 %collective-permute-done.17 = bf16[128,768]{1,0:T(8,128)(2,1)S(1)} collective-permute-done((bf16[128,768]{1,0:T(8,128)(2,1)S(1)}, bf16[128,768]{1,0:T(8,128)(2,1)S(1)}, u32[]{:S(2)}, u32[]{:S(2)}) %collective-permute-start.17) | collective-permute-done | bytes 196640 | tf_op jit(solution)/shard_map/ppermute | solution.py:41
  (545 shorter events, 314.0 us)
Async XLA Ops:
  11.1 131.1 %collective-permute-start.48 = (bf16[256,1024]{1,0:T(8,128)(2,1)}, bf16[256,1024]{1,0:T(8,128)(2,1)}, u32[]{:S(2)}, u32[]{:S(2)}) collective-permute-start(bf16[256,1024]{1,0:T(8,128)(2,1)} %get-tuple-element.108), channel_id=1, source_target_pairs={{0,4},{2,6},{4,0},{6,2},{1,5},{3,7},{5,1},{7,3},{8,12},{10,14},{12... | collective-permute-start | bytes 1572872 | tf_op jit(solution)/shard_map/ppermute | solution.py:41
  18.7 127.8 %collective-permute-start.52 = (bf16[256,1024]{1,0:T(8,128)(2,1)}, bf16[256,1024]{1,0:T(8,128)(2,1)}, u32[]{:S(2)}, u32[]{:S(2)}) collective-permute-start(bf16[256,1024]{1,0:T(8,128)(2,1)} %get-tuple-element.106), channel_id=1, source_target_pairs={{0,4},{2,6},{4,0},{6,2},{1,5},{3,7},{5,1},{7,3},{8,12},{10,14},{12... | collective-permute-start | bytes 1572872 | tf_op jit(solution)/shard_map/ppermute | solution.py:41
  23.3 125.5 %collective-permute-start.56 = (bf16[256,1024]{1,0:T(8,128)(2,1)}, bf16[256,1024]{1,0:T(8,128)(2,1)}, u32[]{:S(2)}, u32[]{:S(2)}) collective-permute-start(bf16[256,1024]{1,0:T(8,128)(2,1)} %get-tuple-element.110), channel_id=1, source_target_pairs={{0,4},{2,6},{4,0},{6,2},{1,5},{3,7},{5,1},{7,3},{8,12},{10,14},{12... | collective-permute-start | bytes 1572872 | tf_op jit(solution)/shard_map/ppermute | solution.py:41
  30.1 123.0 %collective-permute-start.60 = (bf16[256,1024]{1,0:T(8,128)(2,1)}, bf16[256,1024]{1,0:T(8,128)(2,1)}, u32[]{:S(2)}, u32[]{:S(2)}) collective-permute-start(bf16[256,1024]{1,0:T(8,128)(2,1)} %get-tuple-element.112), channel_id=1, source_target_pairs={{0,4},{2,6},{4,0},{6,2},{1,5},{3,7},{5,1},{7,3},{8,12},{10,14},{12... | collective-permute-start | bytes 1572872 | tf_op jit(solution)/shard_map/ppermute | solution.py:41
  30.7 107.6 %collective-permute-start.8 = (f32[1,2,256]{2,1,0:T(2,128)}, f32[1,2,256]{2,1,0:T(2,128)}, u32[]{:S(2)}, u32[]{:S(2)}) collective-permute-start(f32[1,2,256]{2,1,0:T(2,128)} %maximum_bitcast_fusion.9), channel_id=1, source_target_pairs={{0,4},{2,6},{4,0},{6,2},{1,5},{3,7},{5,1},{7,3},{8,12},{10,14},{12... | collective-permute-start | bytes 6152 | tf_op jit(solution)/shard_map/ppermute | solution.py:41
  156.0 81.7 %collective-permute-start = (bf16[256,2,1024]{0,2,1:T(8,128)(2,1)S(1)}, bf16[256,2,1024]{0,2,1:T(8,128)(2,1)S(1)}, u32[]{:S(2)}, u32[]{:S(2)}) collective-permute-start(bf16[256,2,1024]{0,2,1:T(8,128)(2,1)S(1)} %maximum_bitcast_fusion.1), channel_id=1, source_target_pairs={{0,4},{2,6},{4,0},{6,2},{1,5},{3,7},{5,1},{7,3},{8,12},{10,14},{12... | collective-permute-start | bytes 3145736 | tf_op jit(solution)/shard_map/ppermute | solution.py:41
  178.5 55.8 %collective-permute-start.44 = (bf16[256,1024]{1,0:T(8,128)(2,1)S(1)}, bf16[256,1024]{1,0:T(8,128)(2,1)S(1)}, u32[]{:S(2)}, u32[]{:S(2)}) collective-permute-start(bf16[256,1024]{1,0:T(8,128)(2,1)S(1)} %get-tuple-element.115), channel_id=1, source_target_pairs={{0,4},{2,6},{4,0},{6,2},{1,5},{3,7},{5,1},{7,3},{8,12},{10,14},{12... | collective-permute-start | bytes 1572872 | tf_op jit(solution)/shard_map/ppermute | solution.py:41
  189.7 51.6 %collective-permute-start.49 = (bf16[512,1024]{1,0:T(8,128)(2,1)}, bf16[512,1024]{1,0:T(8,128)(2,1)}, u32[]{:S(2)}, u32[]{:S(2)}) collective-permute-start(bf16[512,1024]{1,0:T(8,128)(2,1)} %pad_maximum_fusion.26), channel_id=1, source_target_pairs={{0,2},{2,0},{4,6},{6,4},{1,3},{3,1},{5,7},{7,5},{8,10},{10,8},{12,... | collective-permute-start | bytes 3145736 | tf_op jit(solution)/shard_map/ppermute | solution.py:41
  249.4 159.1 %collective-permute-start.1 = (bf16[512,2,1024]{0,2,1:T(8,128)(2,1)S(1)}, bf16[512,2,1024]{0,2,1:T(8,128)(2,1)S(1)}, u32[]{:S(2)}, u32[]{:S(2)}) collective-permute-start(bf16[512,2,1024]{0,2,1:T(8,128)(2,1)S(1)} %copy-done.12), channel_id=1, source_target_pairs={{0,2},{2,0},{4,6},{6,4},{1,3},{3,1},{5,7},{7,5},{8,10},{10,8},{12,... | collective-permute-start | bytes 6291464 | tf_op jit(solution)/shard_map/ppermute | solution.py:41
  278.0 50.6 %collective-permute-start.38 = (bf16[256,1024]{1,0:T(8,128)(2,1)S(1)}, bf16[256,1024]{1,0:T(8,128)(2,1)S(1)}, u32[]{:S(2)}, u32[]{:S(2)}) collective-permute-start(bf16[256,1024]{1,0:T(8,128)(2,1)S(1)} %convolution_convert_fusion.6), channel_id=1, source_target_pairs={{0,8},{8,0},{16,24},{24,16},{1,9},{9,1},{17,25},{25,17},{2,10},{10... | collective-permute-start | bytes 1572872 | tf_op jit(solution)/shard_map/ppermute | solution.py:41
  289.2 56.2 %collective-permute-start.42 = (bf16[256,1024]{1,0:T(8,128)(2,1)S(1)}, bf16[256,1024]{1,0:T(8,128)(2,1)S(1)}, u32[]{:S(2)}, u32[]{:S(2)}) collective-permute-start(bf16[256,1024]{1,0:T(8,128)(2,1)S(1)} %convolution_convert_fusion.5), channel_id=1, source_target_pairs={{0,8},{8,0},{16,24},{24,16},{1,9},{9,1},{17,25},{25,17},{2,10},{10... | collective-permute-start | bytes 1572872 | tf_op jit(solution)/shard_map/ppermute | solution.py:41
  300.5 55.5 %collective-permute-start.46 = (bf16[256,1024]{1,0:T(8,128)(2,1)S(1)}, bf16[256,1024]{1,0:T(8,128)(2,1)S(1)}, u32[]{:S(2)}, u32[]{:S(2)}) collective-permute-start(bf16[256,1024]{1,0:T(8,128)(2,1)S(1)} %convolution_convert_fusion.4), channel_id=1, source_target_pairs={{0,8},{8,0},{16,24},{24,16},{1,9},{9,1},{17,25},{25,17},{2,10},{10... | collective-permute-start | bytes 1572872 | tf_op jit(solution)/shard_map/ppermute | solution.py:41
  311.7 48.8 %collective-permute-start.51 = (bf16[1024,128]{1,0:T(8,128)(2,1)S(1)}, bf16[1024,128]{1,0:T(8,128)(2,1)S(1)}, u32[]{:S(2)}, u32[]{:S(2)}) collective-permute-start(bf16[1024,128]{1,0:T(8,128)(2,1)S(1)} %slice.843), channel_id=1, source_target_pairs={{0,16},{8,24},{16,0},{24,8},{1,17},{9,25},{17,1},{25,9},{2,18},{10... | collective-permute-start | bytes 786440 | tf_op jit(solution)/shard_map/ppermute | solution.py:41
  362.3 56.0 %collective-permute-start.39 = (bf16[128,1024]{1,0:T(8,128)(2,1)}, bf16[128,1024]{1,0:T(8,128)(2,1)}, u32[]{:S(2)}, u32[]{:S(2)}) collective-permute-start(bf16[128,1024]{1,0:T(8,128)(2,1)} %slice.846), channel_id=1, source_target_pairs={{0,16},{8,24},{16,0},{24,8},{1,17},{9,25},{17,1},{25,9},{2,18},{10... | collective-permute-start | bytes 786440 | tf_op jit(solution)/shard_map/ppermute | solution.py:41
  441.1 48.3 %collective-permute-start.2 = (bf16[256,2048]{1,0:T(8,128)(2,1)}, bf16[256,2048]{1,0:T(8,128)(2,1)}, u32[]{:S(2)}, u32[]{:S(2)}) collective-permute-start(bf16[256,2048]{1,0:T(8,128)(2,1)} %fusion.57), channel_id=1, source_target_pairs={{0,1},{1,0},{2,3},{3,2},{4,5},{5,4},{6,7},{7,6},{8,9},{9,8},{10,11... | collective-permute-start | bytes 3145736 | tf_op jit(solution)/shard_map/ppermute | solution.py:41
  489.0 69.0 %collective-permute-start.10 = (bf16[256,768]{0,1:T(8,128)(2,1)}, bf16[256,768]{0,1:T(8,128)(2,1)}, u32[]{:S(2)}, u32[]{:S(2)}) collective-permute-start(bf16[256,768]{0,1:T(8,128)(2,1)} %get-tuple-element.34), channel_id=1, source_target_pairs={{0,4},{2,6},{4,0},{6,2},{1,5},{3,7},{5,1},{7,3},{8,12},{10,14},{12... | collective-permute-start | bytes 1179656 | tf_op jit(solution)/shard_map/ppermute | solution.py:41
  493.1 72.9 %collective-permute-start.5 = (bf16[256,2048]{1,0:T(8,128)(2,1)S(1)}, bf16[256,2048]{1,0:T(8,128)(2,1)}, u32[]{:S(2)}, u32[]{:S(2)}) collective-permute-start(bf16[256,2048]{1,0:T(8,128)(2,1)S(1)} %get-tuple-element.58), channel_id=1, source_target_pairs={{0,1},{1,0},{2,3},{3,2},{4,5},{5,4},{6,7},{7,6},{8,9},{9,8},{10,11... | collective-permute-start | bytes 3145736 | tf_op jit(solution)/shard_map/ppermute | solution.py:41
  494.7 66.1 %collective-permute-start.14 = (bf16[256,768]{0,1:T(8,128)(2,1)}, bf16[256,768]{0,1:T(8,128)(2,1)S(1)}, u32[]{:S(2)}, u32[]{:S(2)}) collective-permute-start(bf16[256,768]{0,1:T(8,128)(2,1)} %get-tuple-element.37), channel_id=1, source_target_pairs={{0,4},{2,6},{4,0},{6,2},{1,5},{3,7},{5,1},{7,3},{8,12},{10,14},{12... | collective-permute-start | bytes 1179656 | tf_op jit(solution)/shard_map/ppermute | solution.py:41
  496.2 67.3 %collective-permute-start.18 = (bf16[256,768]{0,1:T(8,128)(2,1)S(1)}, bf16[256,768]{0,1:T(8,128)(2,1)S(1)}, u32[]{:S(2)}, u32[]{:S(2)}) collective-permute-start(bf16[256,768]{0,1:T(8,128)(2,1)S(1)} %get-tuple-element.36), channel_id=1, source_target_pairs={{0,4},{2,6},{4,0},{6,2},{1,5},{3,7},{5,1},{7,3},{8,12},{10,14},{12... | collective-permute-start | bytes 1179656 | tf_op jit(solution)/shard_map/ppermute | solution.py:41
  496.7 67.8 %collective-permute-start.22 = (bf16[256,768]{0,1:T(8,128)(2,1)S(1)}, bf16[256,768]{0,1:T(8,128)(2,1)S(1)}, u32[]{:S(2)}, u32[]{:S(2)}) collective-permute-start(bf16[256,768]{0,1:T(8,128)(2,1)S(1)} %get-tuple-element.35), channel_id=1, source_target_pairs={{0,4},{2,6},{4,0},{6,2},{1,5},{3,7},{5,1},{7,3},{8,12},{10,14},{12... | collective-permute-start | bytes 1179656 | tf_op jit(solution)/shard_map/ppermute | solution.py:41
  560.1 70.4 %collective-permute-start.11 = (bf16[512,768]{0,1:T(8,128)(2,1)}, bf16[512,768]{0,1:T(8,128)(2,1)}, u32[]{:S(2)}, u32[]{:S(2)}) collective-permute-start(bf16[512,768]{0,1:T(8,128)(2,1)} %pad_maximum_fusion.48), channel_id=1, source_target_pairs={{0,2},{2,0},{4,6},{6,4},{1,3},{3,1},{5,7},{7,5},{8,10},{10,8},{12,... | collective-permute-start | bytes 2359304 | tf_op jit(solution)/shard_map/ppermute | solution.py:41
  562.9 69.7 %collective-permute-start.15 = (bf16[512,768]{0,1:T(8,128)(2,1)}, bf16[512,768]{0,1:T(8,128)(2,1)}, u32[]{:S(2)}, u32[]{:S(2)}) collective-permute-start(bf16[512,768]{0,1:T(8,128)(2,1)} %pad_maximum_fusion.49), channel_id=1, source_target_pairs={{0,2},{2,0},{4,6},{6,4},{1,3},{3,1},{5,7},{7,5},{8,10},{10,8},{12,... | collective-permute-start | bytes 2359304 | tf_op jit(solution)/shard_map/ppermute | solution.py:41
  564.5 72.1 %collective-permute-start.19 = (bf16[512,768]{0,1:T(8,128)(2,1)}, bf16[512,768]{0,1:T(8,128)(2,1)}, u32[]{:S(2)}, u32[]{:S(2)}) collective-permute-start(bf16[512,768]{0,1:T(8,128)(2,1)} %pad_maximum_fusion.50), channel_id=1, source_target_pairs={{0,2},{2,0},{4,6},{6,4},{1,3},{3,1},{5,7},{7,5},{8,10},{10,8},{12,... | collective-permute-start | bytes 2359304 | tf_op jit(solution)/shard_map/ppermute | solution.py:41
  565.5 73.0 %collective-permute-start.23 = (bf16[512,768]{0,1:T(8,128)(2,1)}, bf16[512,768]{0,1:T(8,128)(2,1)}, u32[]{:S(2)}, u32[]{:S(2)}) collective-permute-start(bf16[512,768]{0,1:T(8,128)(2,1)} %pad_maximum_fusion.51), channel_id=1, source_target_pairs={{0,2},{2,0},{4,6},{6,4},{1,3},{3,1},{5,7},{7,5},{8,10},{10,8},{12,... | collective-permute-start | bytes 2359304 | tf_op jit(solution)/shard_map/ppermute | solution.py:41
  (154 other events, 2057.0 us)
where the time goes:
time: 702 us; the launch traced here: 692 us
  waiting for transfers between devices  248 us (35%)
  matrix products  147 us (21%)
  blocking collectives  121 us (17%)
  other arithmetic  74.1 us (11%)
  starting transfers between devices  51.7 us (7%)
  local copies, waits for them, and re-layouts  46.3 us (7%)
    ppermute x64, waiting for transfers between devices, swap(): return lax.ppermute(array, axis, pairs)  248 us
    psum x1, blocking collectives, local(): lax.psum((grad_qkv_bias, jnp.concatenate(up_bias_parts), grad_out_bias),...  61.6 us
    psum x1, blocking collectives, local(): norm_total = lax.psum(norm_parts, ('dp', 'ctx', 'tensor'))  59.7 us
    ppermute x64, starting transfers between devices, swap(): return lax.ppermute(array, axis, pairs)  51.7 us
    concatenate x16, other arithmetic, gather_rows(): rows = jnp.concatenate([rows, swap(rows, axis, bit)], 0)  24.4 us
    dot_general x13, matrix products, reduce_line(): jnp.einsum(spec, left[:, count * width:], right, preferred_element_type=j...  24 us
    dot_general x13, matrix products, reduce_line(): jnp.einsum(spec, left[:, :count * width], right, preferred_element_type=j...  23.1 us
    dot_general x4, matrix products, local(): jnp.einsum('rd,fd->rf', grad_low, down_weight[cols], preferred_element_ty...  21.9 us
  transfers between devices with their start and end apart: 64, of which 27 were waited for; matrix products, arithmetic and copies ran while one was open for 36% of the time, Pallas kernels for 0%

commit v1 on v0

--- a/solution.py
+++ b/solution.py
@@ -309,7 +309,7 @@
     )
     norm_total = lax.psum(norm_parts, ("dp", "ctx", "tensor"))
     qkv_bias_sum, up_bias_sum, out_bias_sum = lax.psum(
-        (grad_qkv_bias, jnp.concatenate(up_bias_parts), grad_out_bias), ("dp", "ctx")
+        lax.psum((grad_qkv_bias, jnp.concatenate(up_bias_parts), grad_out_bias), "ctx"), "dp"
     )
     return (
         layer_out,

time: 702 us -> 670 us (0.954)
  blocking collectives: 121 us -> 91.2 us
    psum x1, blocking collectives: 61.6 us -> 12.4 us  [local(): lax.psum((grad_qkv_bias, jnp.concatenate(up_bias_parts), grad_out_bias),...]
    psum x0 -> x1, blocking collectives: none -> 19.1 us  [local(): lax.psum(lax.psum((grad_qkv_bias, jnp.concatenate(up_bias_parts), grad_ou...]
  transfers between devices with their start and end apart: 64 -> 64, of which waited for: 27 -> 27; matrix products, arithmetic and copies ran while one was open for 36% -> 38% of each run, Pallas kernels for 0% -> 0%
where the time goes in v1:
time: 670 us; the launch traced here: 660 us
  waiting for transfers between devices  246 us (37%)
  matrix products  147 us (22%)
  blocking collectives  91.2 us (14%)
  other arithmetic  74.1 us (11%)
  starting transfers between devices  51.3 us (8%)
  local copies, waits for them, and re-layouts  46.3 us (7%)
    ppermute x64, waiting for transfers between devices, swap(): return lax.ppermute(array, axis, pairs)  246 us
    psum x1, blocking collectives, local(): norm_total = lax.psum(norm_parts, ('dp', 'ctx', 'tensor'))  59.7 us
    ppermute x64, starting transfers between devices, swap(): return lax.ppermute(array, axis, pairs)  51.3 us
    concatenate x16, other arithmetic, gather_rows(): rows = jnp.concatenate([rows, swap(rows, axis, bit)], 0)  24.5 us
    dot_general x13, matrix products, reduce_line(): jnp.einsum(spec, left[:, count * width:], right, preferred_element_type=j...  24 us
    dot_general x13, matrix products, reduce_line(): jnp.einsum(spec, left[:, :count * width], right, preferred_element_type=j...  23.2 us
    dot_general x4, matrix products, local(): jnp.einsum('rd,fd->rf', grad_low, down_weight[cols], preferred_element_ty...  21.9 us
    dot_general x4, matrix products, local(): jnp.dot(mlp_in, up_weight[:, cols], preferred_element_type=jnp.float32)  20.9 us
  transfers between devices with their start and end apart: 64, of which 27 were waited for; matrix products, arithmetic and copies ran while one was open for 38% of the time, Pallas kernels for 0%

profile of v1, /device:TPU:0, one launch (start us, length us, event | category | flops | bytes accessed | tf_op | source)
XLA Modules:
  0.0 659.5 jit_solution(12211364025811393410)
XLA Ops:
  34.3 9.9 %convolution_add_fusion = f32[256,3072]{1,0:T(8,128)} fusion(bf16[2048,3072]{1,0:T(8,128)(2,1)} %param.19, f32[3072]{0:T(1024)S(1)} %copy-done.93, bf16[1,256,2048]{2,1,0:T(8,128)(2,1)S(1)} %copy-done, f32[2048]{0:T(1024)S(1)} %copy-done.67, f32[2048]{0:T(1024)S(1)} %copy-done.70, f32[256]{0:T(256)S(1)} %add_rsqrt_fusion, f32[256]{0:T(256)S(1)} %broadcast_multiply_fusion.2), kind=kOutput, calls=%fused_computation.12 | convolution fusion | flops 3225157632 | bytes 16807936 | tf_op jit(solution)/shard_map/dot_general | solution.py:215
  85.4 7.3 %convert_reduce_fusion.5 = (f32[1024]{0:T(1024)}, bf16[256,1024]{1,0:T(8,128)(2,1)}) fusion(f32[256,1024]{1,0:T(8,128)S(1)} %copy-done.94, bf16[4096,2048]{1,0:T(8,128)(2,1)} %param.27, bf16[1,256,2048]{2,1,0:T(8,128)(2,1)S(1)} %copy-done.3, f32[256]{0:T(256)S(1)} %fusion.188), kind=kOutput, calls=%fused_computation.202 | convolution fusion | flops 1094712320 | bytes 6820864 | tf_op jit(solution)/shard_map/rd,fd->rf/dot_general | solution.py:201
  158.5 20.1 %collective-permute-done.6 = bf16[256,2,512]{0,2,1:T(8,128)(2,1)S(1)} collective-permute-done((bf16[256,2,512]{0,2,1:T(8,128)(2,1)S(1)}, bf16[256,2,512]{0,2,1:T(8,128)(2,1)S(1)}, u32[]{:S(2)}, u32[]{:S(2)}) %collective-permute-start.6) | collective-permute-done | bytes 524320 | tf_op jit(solution)/shard_map/ppermute | solution.py:41
  178.7 11.0 %collective-permute-done.28 = bf16[256,2,512]{0,2,1:T(8,128)(2,1)S(1)} collective-permute-done((bf16[256,2,512]{0,2,1:T(8,128)(2,1)S(1)}, bf16[256,2,512]{0,2,1:T(8,128)(2,1)S(1)}, u32[]{:S(2)}, u32[]{:S(2)}) %collective-permute-start.28) | collective-permute-done | bytes 524320 | tf_op jit(solution)/shard_map/ppermute | solution.py:41
  191.5 9.5 %collective-permute-done.40 = bf16[256,1024]{1,0:T(8,128)(2,1)S(1)} collective-permute-done((bf16[256,1024]{1,0:T(8,128)(2,1)}, bf16[256,1024]{1,0:T(8,128)(2,1)S(1)}, u32[]{:S(2)}, u32[]{:S(2)}) %collective-permute-start.40) | collective-permute-done | bytes 524320 | tf_op jit(solution)/shard_map/ppermute | solution.py:41
  203.4 31.0 %collective-permute-done.44 = bf16[256,1024]{1,0:T(8,128)(2,1)S(1)} collective-permute-done((bf16[256,1024]{1,0:T(8,128)(2,1)S(1)}, bf16[256,1024]{1,0:T(8,128)(2,1)S(1)}, u32[]{:S(2)}, u32[]{:S(2)}) %collective-permute-start.44) | collective-permute-done | bytes 524320 | tf_op jit(solution)/shard_map/ppermute | solution.py:41
  270.6 7.4 %collective-permute-done.54 = bf16[1024,256]{1,0:T(8,128)(2,1)S(1)} collective-permute-done((bf16[1024,256]{1,0:T(8,128)(2,1)S(1)}, bf16[1024,256]{1,0:T(8,128)(2,1)S(1)}, u32[]{:S(2)}, u32[]{:S(2)}) %collective-permute-start.54) | collective-permute-done | bytes 524320 | tf_op jit(solution)/shard_map/ppermute | solution.py:41
  281.9 7.4 %collective-permute-done.58 = bf16[1024,256]{1,0:T(8,128)(2,1)S(1)} collective-permute-done((bf16[1024,256]{1,0:T(8,128)(2,1)S(1)}, bf16[1024,256]{1,0:T(8,128)(2,1)S(1)}, u32[]{:S(2)}, u32[]{:S(2)}) %collective-permute-start.58) | collective-permute-done | bytes 524320 | tf_op jit(solution)/shard_map/ppermute | solution.py:41
  293.2 7.3 %collective-permute-done.62 = bf16[1024,256]{1,0:T(8,128)(2,1)S(1)} collective-permute-done((bf16[1024,256]{1,0:T(8,128)(2,1)S(1)}, bf16[1024,256]{1,0:T(8,128)(2,1)S(1)}, u32[]{:S(2)}, u32[]{:S(2)}) %collective-permute-start.62) | collective-permute-done | bytes 524320 | tf_op jit(solution)/shard_map/ppermute | solution.py:41
  304.0 7.7 %collective-permute-done.34 = bf16[256,1024]{1,0:T(8,128)(2,1)S(1)} collective-permute-done((bf16[256,1024]{1,0:T(8,128)(2,1)S(1)}, bf16[256,1024]{1,0:T(8,128)(2,1)S(1)}, u32[]{:S(2)}, u32[]{:S(2)}) %collective-permute-start.34) | collective-permute-done | bytes 524320 | tf_op jit(solution)/shard_map/ppermute | solution.py:41
  316.3 12.3 %collective-permute-done.38 = bf16[256,1024]{1,0:T(8,128)(2,1)S(1)} collective-permute-done((bf16[256,1024]{1,0:T(8,128)(2,1)S(1)}, bf16[256,1024]{1,0:T(8,128)(2,1)S(1)}, u32[]{:S(2)}, u32[]{:S(2)}) %collective-permute-start.38) | collective-permute-done | bytes 524320 | tf_op jit(solution)/shard_map/ppermute | solution.py:41
  332.3 13.1 %collective-permute-done.42 = bf16[256,1024]{1,0:T(8,128)(2,1)S(1)} collective-permute-done((bf16[256,1024]{1,0:T(8,128)(2,1)S(1)}, bf16[256,1024]{1,0:T(8,128)(2,1)S(1)}, u32[]{:S(2)}, u32[]{:S(2)}) %collective-permute-start.42) | collective-permute-done | bytes 524320 | tf_op jit(solution)/shard_map/ppermute | solution.py:41
  348.9 7.1 %collective-permute-done.46 = bf16[256,1024]{1,0:T(8,128)(2,1)S(1)} collective-permute-done((bf16[256,1024]{1,0:T(8,128)(2,1)S(1)}, bf16[256,1024]{1,0:T(8,128)(2,1)S(1)}, u32[]{:S(2)}, u32[]{:S(2)}) %collective-permute-start.46) | collective-permute-done | bytes 524320 | tf_op jit(solution)/shard_map/ppermute | solution.py:41
  364.1 21.9 %collective-permute-done.59 = bf16[1024,128]{1,0:T(8,128)(2,1)S(1)} collective-permute-done((bf16[1024,128]{1,0:T(8,128)(2,1)S(1)}, bf16[1024,128]{1,0:T(8,128)(2,1)S(1)}, u32[]{:S(2)}, u32[]{:S(2)}) %collective-permute-start.59) | collective-permute-done | bytes 262176 | tf_op jit(solution)/shard_map/ppermute | solution.py:41
  386.0 11.2 %collective-permute-done.63 = bf16[1024,128]{1,0:T(8,128)(2,1)S(1)} collective-permute-done((bf16[1024,128]{1,0:T(8,128)(2,1)S(1)}, bf16[1024,128]{1,0:T(8,128)(2,1)S(1)}, u32[]{:S(2)}, u32[]{:S(2)}) %collective-permute-start.63) | collective-permute-done | bytes 262176 | tf_op jit(solution)/shard_map/ppermute | solution.py:41
  397.3 11.2 %collective-permute-done.35 = bf16[128,1024]{1,0:T(8,128)(2,1)S(1)} collective-permute-done((bf16[128,1024]{1,0:T(8,128)(2,1)S(1)}, bf16[128,1024]{1,0:T(8,128)(2,1)S(1)}, u32[]{:S(2)}, u32[]{:S(2)}) %collective-permute-start.35) | collective-permute-done | bytes 262176 | tf_op jit(solution)/shard_map/ppermute | solution.py:41
  420.8 8.5 %collective-permute-done.26 = bf16[256,1024]{0,1:T(8,128)(2,1)S(1)} collective-permute-done((bf16[256,1024]{0,1:T(8,128)(2,1)S(1)}, bf16[256,1024]{0,1:T(8,128)(2,1)S(1)}, u32[]{:S(2)}, u32[]{:S(2)}) %collective-permute-start.26) | collective-permute-done | bytes 524320 | tf_op jit(solution)/shard_map/ppermute | solution.py:41
  451.6 12.3 %collective-permute-done.31 = bf16[1024,128]{1,0:T(8,128)(2,1)S(1)} collective-permute-done((bf16[1024,128]{1,0:T(8,128)(2,1)S(1)}, bf16[1024,128]{1,0:T(8,128)(2,1)S(1)}, u32[]{:S(2)}, u32[]{:S(2)}) %collective-permute-start.31) | collective-permute-done | bytes 262176 | tf_op jit(solution)/shard_map/ppermute | solution.py:41
  478.3 9.7 %fusion.236 = (f32[256]{0:T(256)S(1)}, f32[256]{0:T(256)S(1)}, f32[2048]{0:T(1024)S(1)}, f32[2048]{0:T(1024)S(1)}, f32[2048]{0:T(1024)S(1)}, /*index=5*/f32[2048]{0:T(1024)S(1)}, f32[256,2048]{1,0:T(8,128)S(1)}) fusion(f32[256]{0:T(256)S(1)} %copy-done.62, f32[256]{0:T(256)S(1)} %copy-done.54, bf16[1,256,2048]{2,1,0:T(8,128)(2,1)S(1)} %copy-done.1, ...), kind=kOutput, calls=%fused_computation.457 | convolution fusion | flops 3229081088 | bytes 19451904 | tf_op jit(solution)/shard_map/rc,dc->rd/dot_general | solution.py:290
  498.3 59.7 %psum.49 = f32[4,2048]{1,0:T(4,128)S(1)} all-reduce(f32[4,2048]{1,0:T(4,128)S(1)} %pad_maximum_fusion.68), channel_id=1, replica_groups=mesh['dp'=4,'ctx'=4,'tensor'=2] {'dp','ctx','tensor'}, use_global_device_ids=true, to_apply=%region_12.13 | all-reduce | flops 8192 | bytes 65536 | tf_op jit(solution)/shard_map/psum | solution.py:310
  568.9 12.4 %all-reduce = (f32[3072]{0:T(1024)S(1)}, f32[2048]{0:T(1024)S(1)}, f32[4096]{0:T(1024)S(1)}) all-reduce(f32[3072]{0:T(1024)S(1)} %reduce_sum.167, f32[2048]{0:T(1024)S(1)} %get-tuple-element.43, f32[4096]{0:T(1024)S(1)} %pad_maximum_fusion.69), channel_id=1, replica_groups=mesh['dp'=4,'ctx'=4,'tensor'=2] {'ctx'}, use_global_device_ids=true, to_apply=%region_14.15 | all-reduce | flops 9216 | bytes 73728 | tf_op jit(solution)/shard_map/psum | solution.py:312
  581.3 19.1 %all-reduce.1 = (f32[3072]{0:T(1024)}, f32[2048]{0:T(1024)S(1)}, f32[4096]{0:T(1024)}) all-reduce(f32[3072]{0:T(1024)S(1)} %get-tuple-element.24, f32[2048]{0:T(1024)S(1)} %get-tuple-element.25, f32[4096]{0:T(1024)S(1)} %get-tuple-element.26), channel_id=1, replica_groups=mesh['dp'=4,'ctx'=4,'tensor'=2] {'dp'}, use_global_device_ids=true, to_apply=%region_15.16 | all-reduce | flops 9216 | bytes 73728 | tf_op jit(solution)/shard_map/psum | solution.py:311
  620.9 8.8 %collective-permute-done.16 = bf16[256,768]{1,0:T(8,128)(2,1)S(1)} collective-permute-done((bf16[256,768]{1,0:T(8,128)(2,1)S(1)}, bf16[256,768]{1,0:T(8,128)(2,1)S(1)}, u32[]{:S(2)}, u32[]{:S(2)}) %collective-permute-start.16) | collective-permute-done | bytes 393248 | tf_op jit(solution)/shard_map/ppermute | solution.py:41
  631.6 8.3 %collective-permute-done.20 = bf16[256,768]{1,0:T(8,128)(2,1)S(1)} collective-permute-done((bf16[256,768]{1,0:T(8,128)(2,1)S(1)}, bf16[256,768]{1,0:T(8,128)(2,1)S(1)}, u32[]{:S(2)}, u32[]{:S(2)}) %collective-permute-start.20) | collective-permute-done | bytes 393248 | tf_op jit(solution)/shard_map/ppermute | solution.py:41
  (546 shorter events, 322.2 us)
Async XLA Ops:
  11.1 131.1 %collective-permute-start.48 = (bf16[256,1024]{1,0:T(8,128)(2,1)}, bf16[256,1024]{1,0:T(8,128)(2,1)}, u32[]{:S(2)}, u32[]{:S(2)}) collective-permute-start(bf16[256,1024]{1,0:T(8,128)(2,1)} %get-tuple-element.111), channel_id=1, source_target_pairs={{0,4},{2,6},{4,0},{6,2},{1,5},{3,7},{5,1},{7,3},{8,12},{10,14},{12... | collective-permute-start | bytes 1572872 | tf_op jit(solution)/shard_map/ppermute | solution.py:41
  18.7 127.8 %collective-permute-start.52 = (bf16[256,1024]{1,0:T(8,128)(2,1)}, bf16[256,1024]{1,0:T(8,128)(2,1)}, u32[]{:S(2)}, u32[]{:S(2)}) collective-permute-start(bf16[256,1024]{1,0:T(8,128)(2,1)} %get-tuple-element.109), channel_id=1, source_target_pairs={{0,4},{2,6},{4,0},{6,2},{1,5},{3,7},{5,1},{7,3},{8,12},{10,14},{12... | collective-permute-start | bytes 1572872 | tf_op jit(solution)/shard_map/ppermute | solution.py:41
  23.3 125.5 %collective-permute-start.56 = (bf16[256,1024]{1,0:T(8,128)(2,1)}, bf16[256,1024]{1,0:T(8,128)(2,1)}, u32[]{:S(2)}, u32[]{:S(2)}) collective-permute-start(bf16[256,1024]{1,0:T(8,128)(2,1)} %get-tuple-element.113), channel_id=1, source_target_pairs={{0,4},{2,6},{4,0},{6,2},{1,5},{3,7},{5,1},{7,3},{8,12},{10,14},{12... | collective-permute-start | bytes 1572872 | tf_op jit(solution)/shard_map/ppermute | solution.py:41
  30.1 122.9 %collective-permute-start.60 = (bf16[256,1024]{1,0:T(8,128)(2,1)}, bf16[256,1024]{1,0:T(8,128)(2,1)}, u32[]{:S(2)}, u32[]{:S(2)}) collective-permute-start(bf16[256,1024]{1,0:T(8,128)(2,1)} %get-tuple-element.115), channel_id=1, source_target_pairs={{0,4},{2,6},{4,0},{6,2},{1,5},{3,7},{5,1},{7,3},{8,12},{10,14},{12... | collective-permute-start | bytes 1572872 | tf_op jit(solution)/shard_map/ppermute | solution.py:41
  30.7 107.6 %collective-permute-start.8 = (f32[1,2,256]{2,1,0:T(2,128)}, f32[1,2,256]{2,1,0:T(2,128)}, u32[]{:S(2)}, u32[]{:S(2)}) collective-permute-start(f32[1,2,256]{2,1,0:T(2,128)} %maximum_bitcast_fusion.9), channel_id=1, source_target_pairs={{0,4},{2,6},{4,0},{6,2},{1,5},{3,7},{5,1},{7,3},{8,12},{10,14},{12... | collective-permute-start | bytes 6152 | tf_op jit(solution)/shard_map/ppermute | solution.py:41
  142.2 47.6 %collective-permute-start.36 = (bf16[256,1024]{1,0:T(8,128)(2,1)}, bf16[256,1024]{1,0:T(8,128)(2,1)S(1)}, u32[]{:S(2)}, u32[]{:S(2)}) collective-permute-start(bf16[256,1024]{1,0:T(8,128)(2,1)} %get-tuple-element.122), channel_id=1, source_target_pairs={{0,4},{2,6},{4,0},{6,2},{1,5},{3,7},{5,1},{7,3},{8,12},{10,14},{12... | collective-permute-start | bytes 1572872 | tf_op jit(solution)/shard_map/ppermute | solution.py:41
  153.1 48.0 %collective-permute-start.40 = (bf16[256,1024]{1,0:T(8,128)(2,1)}, bf16[256,1024]{1,0:T(8,128)(2,1)S(1)}, u32[]{:S(2)}, u32[]{:S(2)}) collective-permute-start(bf16[256,1024]{1,0:T(8,128)(2,1)} %get-tuple-element.120), channel_id=1, source_target_pairs={{0,4},{2,6},{4,0},{6,2},{1,5},{3,7},{5,1},{7,3},{8,12},{10,14},{12... | collective-permute-start | bytes 1572872 | tf_op jit(solution)/shard_map/ppermute | solution.py:41
  156.1 81.7 %collective-permute-start = (bf16[256,2,1024]{0,2,1:T(8,128)(2,1)S(1)}, bf16[256,2,1024]{0,2,1:T(8,128)(2,1)S(1)}, u32[]{:S(2)}, u32[]{:S(2)}) collective-permute-start(bf16[256,2,1024]{0,2,1:T(8,128)(2,1)S(1)} %maximum_bitcast_fusion.1), channel_id=1, source_target_pairs={{0,4},{2,6},{4,0},{6,2},{1,5},{3,7},{5,1},{7,3},{8,12},{10,14},{12... | collective-permute-start | bytes 3145736 | tf_op jit(solution)/shard_map/ppermute | solution.py:41
  178.6 55.8 %collective-permute-start.44 = (bf16[256,1024]{1,0:T(8,128)(2,1)S(1)}, bf16[256,1024]{1,0:T(8,128)(2,1)S(1)}, u32[]{:S(2)}, u32[]{:S(2)}) collective-permute-start(bf16[256,1024]{1,0:T(8,128)(2,1)S(1)} %get-tuple-element.118), channel_id=1, source_target_pairs={{0,4},{2,6},{4,0},{6,2},{1,5},{3,7},{5,1},{7,3},{8,12},{10,14},{12... | collective-permute-start | bytes 1572872 | tf_op jit(solution)/shard_map/ppermute | solution.py:41
  189.8 51.6 %collective-permute-start.49 = (bf16[512,1024]{1,0:T(8,128)(2,1)}, bf16[512,1024]{1,0:T(8,128)(2,1)}, u32[]{:S(2)}, u32[]{:S(2)}) collective-permute-start(bf16[512,1024]{1,0:T(8,128)(2,1)} %pad_maximum_fusion.26), channel_id=1, source_target_pairs={{0,2},{2,0},{4,6},{6,4},{1,3},{3,1},{5,7},{7,5},{8,10},{10,8},{12,... | collective-permute-start | bytes 3145736 | tf_op jit(solution)/shard_map/ppermute | solution.py:41
  189.8 45.7 %collective-permute-start.7 = (bf16[512,1,512]{0,2,1:T(8,128)(2,1)S(1)}, bf16[512,1,512]{0,2,1:T(8,128)(2,1)S(1)}, u32[]{:S(2)}, u32[]{:S(2)}) collective-permute-start(bf16[512,1,512]{0,2,1:T(8,128)(2,1)S(1)} %get-tuple-element.54), channel_id=1, source_target_pairs={{0,2},{2,0},{4,6},{6,4},{1,3},{3,1},{5,7},{7,5},{8,10},{10,8},{12,... | collective-permute-start | bytes 1572872 | tf_op jit(solution)/shard_map/ppermute | solution.py:41
  249.4 159.1 %collective-permute-start.1 = (bf16[512,2,1024]{0,2,1:T(8,128)(2,1)S(1)}, bf16[512,2,1024]{0,2,1:T(8,128)(2,1)S(1)}, u32[]{:S(2)}, u32[]{:S(2)}) collective-permute-start(bf16[512,2,1024]{0,2,1:T(8,128)(2,1)S(1)} %copy-done.12), channel_id=1, source_target_pairs={{0,2},{2,0},{4,6},{6,4},{1,3},{3,1},{5,7},{7,5},{8,10},{10,8},{12,... | collective-permute-start | bytes 6291464 | tf_op jit(solution)/shard_map/ppermute | solution.py:41
  278.0 50.6 %collective-permute-start.38 = (bf16[256,1024]{1,0:T(8,128)(2,1)S(1)}, bf16[256,1024]{1,0:T(8,128)(2,1)S(1)}, u32[]{:S(2)}, u32[]{:S(2)}) collective-permute-start(bf16[256,1024]{1,0:T(8,128)(2,1)S(1)} %convolution_convert_fusion.6), channel_id=1, source_target_pairs={{0,8},{8,0},{16,24},{24,16},{1,9},{9,1},{17,25},{25,17},{2,10},{10... | collective-permute-start | bytes 1572872 | tf_op jit(solution)/shard_map/ppermute | solution.py:41
  289.3 56.2 %collective-permute-start.42 = (bf16[256,1024]{1,0:T(8,128)(2,1)S(1)}, bf16[256,1024]{1,0:T(8,128)(2,1)S(1)}, u32[]{:S(2)}, u32[]{:S(2)}) collective-permute-start(bf16[256,1024]{1,0:T(8,128)(2,1)S(1)} %convolution_convert_fusion.5), channel_id=1, source_target_pairs={{0,8},{8,0},{16,24},{24,16},{1,9},{9,1},{17,25},{25,17},{2,10},{10... | collective-permute-start | bytes 1572872 | tf_op jit(solution)/shard_map/ppermute | solution.py:41
  300.5 55.5 %collective-permute-start.46 = (bf16[256,1024]{1,0:T(8,128)(2,1)S(1)}, bf16[256,1024]{1,0:T(8,128)(2,1)S(1)}, u32[]{:S(2)}, u32[]{:S(2)}) collective-permute-start(bf16[256,1024]{1,0:T(8,128)(2,1)S(1)} %convolution_convert_fusion.4), channel_id=1, source_target_pairs={{0,8},{8,0},{16,24},{24,16},{1,9},{9,1},{17,25},{25,17},{2,10},{10... | collective-permute-start | bytes 1572872 | tf_op jit(solution)/shard_map/ppermute | solution.py:41
  311.7 48.8 %collective-permute-start.51 = (bf16[1024,128]{1,0:T(8,128)(2,1)S(1)}, bf16[1024,128]{1,0:T(8,128)(2,1)S(1)}, u32[]{:S(2)}, u32[]{:S(2)}) collective-permute-start(bf16[1024,128]{1,0:T(8,128)(2,1)S(1)} %slice.843), channel_id=1, source_target_pairs={{0,16},{8,24},{16,0},{24,8},{1,17},{9,25},{17,1},{25,9},{2,18},{10... | collective-permute-start | bytes 786440 | tf_op jit(solution)/shard_map/ppermute | solution.py:41
  360.5 47.9 %collective-permute-start.35 = (bf16[128,1024]{1,0:T(8,128)(2,1)S(1)}, bf16[128,1024]{1,0:T(8,128)(2,1)S(1)}, u32[]{:S(2)}, u32[]{:S(2)}) collective-permute-start(bf16[128,1024]{1,0:T(8,128)(2,1)S(1)} %slice.847), channel_id=1, source_target_pairs={{0,16},{8,24},{16,0},{24,8},{1,17},{9,25},{17,1},{25,9},{2,18},{10... | collective-permute-start | bytes 786440 | tf_op jit(solution)/shard_map/ppermute | solution.py:41
  362.4 56.0 %collective-permute-start.39 = (bf16[128,1024]{1,0:T(8,128)(2,1)}, bf16[128,1024]{1,0:T(8,128)(2,1)}, u32[]{:S(2)}, u32[]{:S(2)}) collective-permute-start(bf16[128,1024]{1,0:T(8,128)(2,1)} %slice.846), channel_id=1, source_target_pairs={{0,16},{8,24},{16,0},{24,8},{1,17},{9,25},{17,1},{25,9},{2,18},{10... | collective-permute-start | bytes 786440 | tf_op jit(solution)/shard_map/ppermute | solution.py:41
  441.2 48.2 %collective-permute-start.2 = (bf16[256,2048]{1,0:T(8,128)(2,1)}, bf16[256,2048]{1,0:T(8,128)(2,1)}, u32[]{:S(2)}, u32[]{:S(2)}) collective-permute-start(bf16[256,2048]{1,0:T(8,128)(2,1)} %fusion.57), channel_id=1, source_target_pairs={{0,1},{1,0},{2,3},{3,2},{4,5},{5,4},{6,7},{7,6},{8,9},{9,8},{10,11... | collective-permute-start | bytes 3145736 | tf_op jit(solution)/shard_map/ppermute | solution.py:41
  489.0 69.0 %collective-permute-start.10 = (bf16[256,768]{0,1:T(8,128)(2,1)}, bf16[256,768]{0,1:T(8,128)(2,1)}, u32[]{:S(2)}, u32[]{:S(2)}) collective-permute-start(bf16[256,768]{0,1:T(8,128)(2,1)} %get-tuple-element.37), channel_id=1, source_target_pairs={{0,4},{2,6},{4,0},{6,2},{1,5},{3,7},{5,1},{7,3},{8,12},{10,14},{12... | collective-permute-start | bytes 1179656 | tf_op jit(solution)/shard_map/ppermute | solution.py:41
  493.1 73.0 %collective-permute-start.5 = (bf16[256,2048]{1,0:T(8,128)(2,1)S(1)}, bf16[256,2048]{1,0:T(8,128)(2,1)}, u32[]{:S(2)}, u32[]{:S(2)}) collective-permute-start(bf16[256,2048]{1,0:T(8,128)(2,1)S(1)} %get-tuple-element.61), channel_id=1, source_target_pairs={{0,1},{1,0},{2,3},{3,2},{4,5},{5,4},{6,7},{7,6},{8,9},{9,8},{10,11... | collective-permute-start | bytes 3145736 | tf_op jit(solution)/shard_map/ppermute | solution.py:41
  494.7 66.1 %collective-permute-start.14 = (bf16[256,768]{0,1:T(8,128)(2,1)}, bf16[256,768]{0,1:T(8,128)(2,1)S(1)}, u32[]{:S(2)}, u32[]{:S(2)}) collective-permute-start(bf16[256,768]{0,1:T(8,128)(2,1)} %get-tuple-element.40), channel_id=1, source_target_pairs={{0,4},{2,6},{4,0},{6,2},{1,5},{3,7},{5,1},{7,3},{8,12},{10,14},{12... | collective-permute-start | bytes 1179656 | tf_op jit(solution)/shard_map/ppermute | solution.py:41
  496.2 67.3 %collective-permute-start.18 = (bf16[256,768]{0,1:T(8,128)(2,1)S(1)}, bf16[256,768]{0,1:T(8,128)(2,1)S(1)}, u32[]{:S(2)}, u32[]{:S(2)}) collective-permute-start(bf16[256,768]{0,1:T(8,128)(2,1)S(1)} %get-tuple-element.39), channel_id=1, source_target_pairs={{0,4},{2,6},{4,0},{6,2},{1,5},{3,7},{5,1},{7,3},{8,12},{10,14},{12... | collective-permute-start | bytes 1179656 | tf_op jit(solution)/shard_map/ppermute | solution.py:41
  496.7 67.8 %collective-permute-start.22 = (bf16[256,768]{0,1:T(8,128)(2,1)S(1)}, bf16[256,768]{0,1:T(8,128)(2,1)S(1)}, u32[]{:S(2)}, u32[]{:S(2)}) collective-permute-start(bf16[256,768]{0,1:T(8,128)(2,1)S(1)} %get-tuple-element.38), channel_id=1, source_target_pairs={{0,4},{2,6},{4,0},{6,2},{1,5},{3,7},{5,1},{7,3},{8,12},{10,14},{12... | collective-permute-start | bytes 1179656 | tf_op jit(solution)/shard_map/ppermute | solution.py:41
  (154 other events, 1969.1 us)
